TPU v7x, 256 devices: a whole 4x4x8 slice. The times are simulated.
256 devices in a mesh: ctx: 16 (over z, core), head: 8 (over y, x_lo), dp: 2 (over x_hi).
Axes of the slice: x: 4 (x_hi: 2, x_lo: 2; x = x_hi * 2 + x_lo), y: 4, z: 8, core: 2. Of those that a mesh axis runs over, the one named last changes fastest.
Arguments:
- queries: bfloat16 [32768, 5120], P(('dp', 'ctx', 'head')), parts along dimension 0, may hold values from -64 to 64
- keys: bfloat16 [32768, 1024], P(('dp', 'ctx', 'head')), parts along dimension 0, may hold values from -4 to 4
- values: bfloat16 [32768, 1024], P(('dp', 'ctx', 'head')), parts along dimension 0, may hold values from -6 to 6
- doc_lengths: int32 [16], P('dp'), parts along dimension 0, may hold values from 1 to 9216, 16384 in all
- steering: float32 [5120], replicated, may hold values from -3 to 3
Outputs:
- steered: bfloat16 [32768, 5120], P(('dp', 'ctx', 'head')), parts along dimension 0
There are 2 independent parts, one for each index of `dp`. A program takes and returns all parts, laid end to end along the dimension named above; an argument that names none is the same for every part. Nothing has to cross between parts.
Inputs may be any that keep to these rules, and one draw needn't show every extreme that they name: `doc_lengths`: the lengths sum to 16384.
All inputs are finite; a program needn't handle non-finite values.
Results may differ from a plain program's by a relative error of at most 0.0043.
Values may be sent and summed in bfloat16 or wider, within the bound.
No kernel may reach another device: no remote copies, remote signals or barrier semaphores. Data moves between devices by JAX's collectives and lax.ppermute only.
A program may use at most 64 MiB of HBM per device.

v0:
```python
import jax
import jax.numpy as jnp
from jax import lax
from jax.sharding import PartitionSpec as P

QH = 40
KVH = 8
HD = 128


NEG_FILL = -1e30


def doc_index(positions, bounds):
    return jnp.sum((positions[:, None] >= bounds[None, :]).astype(jnp.int32), axis=1)


def fold_panel(running, query_heads, panel, key_start, bounds, query_base):
    row_count, locals_kv, groups, head_dim = query_heads.shape
    panel_rows = panel.shape[0]
    q_block = min(512, row_count)
    k_block = min(1024, panel_rows)
    score_scale = head_dim ** (-0.5)
    key_heads = panel[:, 0].reshape(panel_rows, locals_kv, head_dim)
    value_heads = panel[:, 1].reshape(panel_rows, locals_kv, head_dim)

    def query_step(q_index, current):
        run_max, run_sum, accum = current
        q_start = q_index * q_block
        query_tile = lax.dynamic_slice_in_dim(query_heads, q_start, q_block, 0)
        q_positions = query_base + q_start + jnp.arange(q_block, dtype=jnp.int32)
        q_docs = doc_index(q_positions, bounds)
        partial_value = (
            lax.dynamic_slice_in_dim(run_max, q_start, q_block, 0),
            lax.dynamic_slice_in_dim(run_sum, q_start, q_block, 0),
            lax.dynamic_slice_in_dim(accum, q_start, q_block, 0),
        )

        def key_step(k_index, partial_value):
            k_start = k_index * k_block
            k_positions = k_start + jnp.arange(k_block, dtype=jnp.int32)
            k_docs = doc_index(k_positions, bounds)
            nothing_seen = (
                (k_positions[0] > q_positions[-1]) | (k_docs[-1] < q_docs[0]) | (key_start < 0)
            )

            def update(partial_value):
                blk_max, blk_sum, blk_acc = partial_value
                key_tile = lax.dynamic_slice_in_dim(key_heads, k_start, k_block, 0)
                value_tile = lax.dynamic_slice_in_dim(value_heads, k_start, k_block, 0)
                scores = (
                    jnp.einsum(
                        "qhgd,khd->qhgk", query_tile, key_tile, preferred_element_type=jnp.float32
                    )
                    * score_scale
                )
                visible = (q_docs[:, None] == k_docs[None, :]) & (
                    k_positions[None, :] <= q_positions[:, None]
                )
                visible = visible[:, None, None, :]
                tile_max = jnp.max(jnp.where(visible, scores, NEG_FILL), axis=3)
                new_max = jnp.maximum(blk_max, tile_max)
                weights = jnp.where(visible, jnp.exp(scores - new_max[..., None]), 0.0)
                factor = jnp.exp(blk_max - new_max)
                new_sum = blk_sum * factor + jnp.sum(weights, axis=3)
                product = jnp.einsum(
                    "qhgk,khd->qhgd",
                    weights.astype(jnp.bfloat16),
                    value_tile,
                    preferred_element_type=jnp.float32,
                )
                new_acc = blk_acc * factor[..., None] + product
                return (new_max, new_sum, new_acc)

            return lax.cond(nothing_seen, lambda kept: kept, update, partial_value)

        blk_max, blk_sum, blk_acc = lax.fori_loop(0, panel_rows // k_block, key_step, partial_value)
        return (
            lax.dynamic_update_slice_in_dim(run_max, blk_max, q_start, 0),
            lax.dynamic_update_slice_in_dim(run_sum, blk_sum, q_start, 0),
            lax.dynamic_update_slice_in_dim(accum, blk_acc, q_start, 0),
        )

    return lax.fori_loop(0, row_count // q_block, query_step, running)


def body(queries, keys, values, doc_lengths, steering):
    tok_rows, q_width = queries.shape
    heads_split = lax.axis_size("head")
    locals_kv = KVH // heads_split
    groups = QH // KVH
    paired = jnp.stack((keys, values), axis=1)
    wide_queries = queries.reshape(tok_rows, 1, q_width)
    q_local, kv_local = (
        lax.all_to_all(wide_queries, "head", split_axis=2, concat_axis=0, tiled=True),
        lax.all_to_all(paired, "head", split_axis=2, concat_axis=0, tiled=True),
    )
    row_count = q_local.shape[0]
    query_heads = q_local.reshape(row_count, locals_kv, groups, HD)
    bounds = jnp.cumsum(doc_lengths)
    query_base = lax.axis_index("ctx") * row_count
    running = (
        jnp.full((row_count, locals_kv, groups), NEG_FILL, jnp.float32),
        jnp.zeros((row_count, locals_kv, groups), jnp.float32),
        jnp.zeros((row_count, locals_kv, groups, HD), jnp.float32),
    )
    running = fold_panel(
        running,
        query_heads,
        lax.all_gather(kv_local, "ctx", axis=0, tiled=True),
        jnp.int32(0),
        bounds,
        query_base,
    )
    run_max, run_sum, accum = running
    attended = (
        (accum / run_sum[..., None]).reshape(row_count, q_width // heads_split).astype(jnp.bfloat16)
    )
    token_major = lax.all_to_all(attended, "head", split_axis=0, concat_axis=1, tiled=True)
    return (token_major.astype(jnp.float32) + steering[None, :]).astype(jnp.bfloat16)


def solution(mesh):
    in_specs = (
        P(("dp", "ctx", "head"), None),
        P(("dp", "ctx", "head"), None),
        P(("dp", "ctx", "head"), None),
        P("dp"),
        P(),
    )
    out_specs = P(("dp", "ctx", "head"), None)
    return jax.shard_map(body, mesh=mesh, in_specs=in_specs, out_specs=out_specs, check_vma=False)
```

profile of v0, /device:TPU:225, one launch (start us, length us, event | category | flops | bytes accessed | tf_op | source)
XLA Modules:
  0.0 470.6 jit_solution(7612148928791317944)
XLA Ops:
  8.0 14.1 %all_to_all.43 = bf16[128,2,1024]{0,1,2:T(2,128)(2,1)S(1)} all-to-all(bf16[128,2,1024]{0,1,2:T(2,128)(2,1)S(1)} %copy.38), channel_id=1, replica_groups=mesh['ctx'=16,'head'=8,'dp'=2] {'head'}, dimensions={2} | all-to-all | bytes 1048576 | tf_op jit(solution)/shard_map/all_to_all | solution.py:96
  28.9 28.8 %reduce.2 = bf16[5120,128]{1,0:T(8,128)(2,1)} reduce(bf16[5120,1,128]{2,1,0:T(2,128)(2,1)S(1)} %bitcast.97, bf16[]{:T(256)} %broadcast.62), dimensions={1}, to_apply=%bitcast.86.reduce_sub_computation | reduce | bytes 2621442
  66.4 16.0 %all-to-all-done = bf16[8,2,40960]{2,1,0:T(2,128)(2,1)} async-done(((bf16[8,2,40960]{2,1,0:T(2,128)(2,1)}), bf16[8,2,40960]{2,1,0:T(2,128)(2,1)}, u32[]{:S(2)}, u32[]{:S(2)}) %all-to-all-start) | async-done | bytes 1310752 | tf_op jit(solution)/shard_map/all_to_all | solution.py:95
  102.7 336.8 %while.55 = (s32[]{:T(128)}, f32[1024,1,5]{0,2,1:T(8,128)S(1)}, f32[1024,1,5]{0,2,1:T(8,128)S(1)}, f32[1024,1,5,128]{0,3,2,1:T(8,128)}, s32[]{:T(128)}, /*index=...) while((s32[]{:T(128)}, f32[1024,1,5]{0,2,1:T(8,128)S(1)}, ...), condition=%wide.region_10.11_spmd, body=%wide.region_1.10_spmd.sunk | while | flops 1373285888 | bytes 45521656 | solution.py:84
  104.7 165.1 %while.56 = (s32[]{:T(128)}, f32[512,1,5]{0,2,1:T(8,128)S(1)}, f32[512,1,5]{0,2,1:T(8,128)S(1)}, f32[512,1,5,128]{0,3,2,1:T(8,128)S(1)}, s32[512]{0:T(512)S(1)},...) while((s32[]{:T(128)}, f32[512,1,5]{0,2,1:T(8,128)S(1)}, ...), condition=%wide.region_9.9_spmd, body=%wide.region_3.8_spmd.sunk | while | flops 1373273600 | bytes 37544336 | solution.py:77
  144.0 9.6 %conditional.2 = (f32[512,1,5]{0,2,1:T(8,128)S(1)}, f32[512,1,5]{0,2,1:T(8,128)S(1)}, f32[512,1,5,128]{0,3,2,1:T(8,128)S(1)}) conditional(s32[]{:T(128)} %bitcast.94, (s32[512]{0:T(512)S(1)}, s32[1024]{0:T(1024)S(1)}, s32[1024]{0:T(1024)S(1)}, s32[512]{0:T(512)S(1)}, s32[]{:T(128)}, /*index=5*/bf16[16384,1,128]{2,0,1:T(8,128)(2,1)}, ...), branch_computations={%region_5.6_spmd, %region_8.7_spmd} | conditional | flops 1373249024 | bytes 37511232 | solution.py:75
  158.6 9.6 %conditional.2 = (f32[512,1,5]{0,2,1:T(8,128)S(1)}, f32[512,1,5]{0,2,1:T(8,128)S(1)}, f32[512,1,5,128]{0,3,2,1:T(8,128)S(1)}) conditional(s32[]{:T(128)} %bitcast.94, (s32[512]{0:T(512)S(1)}, s32[1024]{0:T(1024)S(1)}, s32[1024]{0:T(1024)S(1)}, s32[512]{0:T(512)S(1)}, s32[]{:T(128)}, /*index=5*/bf16[16384,1,128]{2,0,1:T(8,128)(2,1)}, ...), branch_computations={%region_5.6_spmd, %region_8.7_spmd} | conditional | flops 1373249024 | bytes 37511232 | solution.py:75
  173.1 9.6 %conditional.2 = (f32[512,1,5]{0,2,1:T(8,128)S(1)}, f32[512,1,5]{0,2,1:T(8,128)S(1)}, f32[512,1,5,128]{0,3,2,1:T(8,128)S(1)}) conditional(s32[]{:T(128)} %bitcast.94, (s32[512]{0:T(512)S(1)}, s32[1024]{0:T(1024)S(1)}, s32[1024]{0:T(1024)S(1)}, s32[512]{0:T(512)S(1)}, s32[]{:T(128)}, /*index=5*/bf16[16384,1,128]{2,0,1:T(8,128)(2,1)}, ...), branch_computations={%region_5.6_spmd, %region_8.7_spmd} | conditional | flops 1373249024 | bytes 37511232 | solution.py:75
  187.6 9.6 %conditional.2 = (f32[512,1,5]{0,2,1:T(8,128)S(1)}, f32[512,1,5]{0,2,1:T(8,128)S(1)}, f32[512,1,5,128]{0,3,2,1:T(8,128)S(1)}) conditional(s32[]{:T(128)} %bitcast.94, (s32[512]{0:T(512)S(1)}, s32[1024]{0:T(1024)S(1)}, s32[1024]{0:T(1024)S(1)}, s32[512]{0:T(512)S(1)}, s32[]{:T(128)}, /*index=5*/bf16[16384,1,128]{2,0,1:T(8,128)(2,1)}, ...), branch_computations={%region_5.6_spmd, %region_8.7_spmd} | conditional | flops 1373249024 | bytes 37511232 | solution.py:75
  202.1 9.6 %conditional.2 = (f32[512,1,5]{0,2,1:T(8,128)S(1)}, f32[512,1,5]{0,2,1:T(8,128)S(1)}, f32[512,1,5,128]{0,3,2,1:T(8,128)S(1)}) conditional(s32[]{:T(128)} %bitcast.94, (s32[512]{0:T(512)S(1)}, s32[1024]{0:T(1024)S(1)}, s32[1024]{0:T(1024)S(1)}, s32[512]{0:T(512)S(1)}, s32[]{:T(128)}, /*index=5*/bf16[16384,1,128]{2,0,1:T(8,128)(2,1)}, ...), branch_computations={%region_5.6_spmd, %region_8.7_spmd} | conditional | flops 1373249024 | bytes 37511232 | solution.py:75
  216.6 9.6 %conditional.2 = (f32[512,1,5]{0,2,1:T(8,128)S(1)}, f32[512,1,5]{0,2,1:T(8,128)S(1)}, f32[512,1,5,128]{0,3,2,1:T(8,128)S(1)}) conditional(s32[]{:T(128)} %bitcast.94, (s32[512]{0:T(512)S(1)}, s32[1024]{0:T(1024)S(1)}, s32[1024]{0:T(1024)S(1)}, s32[512]{0:T(512)S(1)}, s32[]{:T(128)}, /*index=5*/bf16[16384,1,128]{2,0,1:T(8,128)(2,1)}, ...), branch_computations={%region_5.6_spmd, %region_8.7_spmd} | conditional | flops 1373249024 | bytes 37511232 | solution.py:75
  231.2 9.6 %conditional.2 = (f32[512,1,5]{0,2,1:T(8,128)S(1)}, f32[512,1,5]{0,2,1:T(8,128)S(1)}, f32[512,1,5,128]{0,3,2,1:T(8,128)S(1)}) conditional(s32[]{:T(128)} %bitcast.94, (s32[512]{0:T(512)S(1)}, s32[1024]{0:T(1024)S(1)}, s32[1024]{0:T(1024)S(1)}, s32[512]{0:T(512)S(1)}, s32[]{:T(128)}, /*index=5*/bf16[16384,1,128]{2,0,1:T(8,128)(2,1)}, ...), branch_computations={%region_5.6_spmd, %region_8.7_spmd} | conditional | flops 1373249024 | bytes 37511232 | solution.py:75
  245.7 9.6 %conditional.2 = (f32[512,1,5]{0,2,1:T(8,128)S(1)}, f32[512,1,5]{0,2,1:T(8,128)S(1)}, f32[512,1,5,128]{0,3,2,1:T(8,128)S(1)}) conditional(s32[]{:T(128)} %bitcast.94, (s32[512]{0:T(512)S(1)}, s32[1024]{0:T(1024)S(1)}, s32[1024]{0:T(1024)S(1)}, s32[512]{0:T(512)S(1)}, s32[]{:T(128)}, /*index=5*/bf16[16384,1,128]{2,0,1:T(8,128)(2,1)}, ...), branch_computations={%region_5.6_spmd, %region_8.7_spmd} | conditional | flops 1373249024 | bytes 37511232 | solution.py:75
  260.2 9.6 %conditional.2 = (f32[512,1,5]{0,2,1:T(8,128)S(1)}, f32[512,1,5]{0,2,1:T(8,128)S(1)}, f32[512,1,5,128]{0,3,2,1:T(8,128)S(1)}) conditional(s32[]{:T(128)} %bitcast.94, (s32[512]{0:T(512)S(1)}, s32[1024]{0:T(1024)S(1)}, s32[1024]{0:T(1024)S(1)}, s32[512]{0:T(512)S(1)}, s32[]{:T(128)}, /*index=5*/bf16[16384,1,128]{2,0,1:T(8,128)(2,1)}, ...), branch_computations={%region_5.6_spmd, %region_8.7_spmd} | conditional | flops 1373249024 | bytes 37511232 | solution.py:75
  273.1 165.1 %while.56 = (s32[]{:T(128)}, f32[512,1,5]{0,2,1:T(8,128)S(1)}, f32[512,1,5]{0,2,1:T(8,128)S(1)}, f32[512,1,5,128]{0,3,2,1:T(8,128)S(1)}, s32[512]{0:T(512)S(1)},...) while((s32[]{:T(128)}, f32[512,1,5]{0,2,1:T(8,128)S(1)}, ...), condition=%wide.region_9.9_spmd, body=%wide.region_3.8_spmd.sunk | while | flops 1373273600 | bytes 37544336 | solution.py:77
  327.0 9.6 %conditional.2 = (f32[512,1,5]{0,2,1:T(8,128)S(1)}, f32[512,1,5]{0,2,1:T(8,128)S(1)}, f32[512,1,5,128]{0,3,2,1:T(8,128)S(1)}) conditional(s32[]{:T(128)} %bitcast.94, (s32[512]{0:T(512)S(1)}, s32[1024]{0:T(1024)S(1)}, s32[1024]{0:T(1024)S(1)}, s32[512]{0:T(512)S(1)}, s32[]{:T(128)}, /*index=5*/bf16[16384,1,128]{2,0,1:T(8,128)(2,1)}, ...), branch_computations={%region_5.6_spmd, %region_8.7_spmd} | conditional | flops 1373249024 | bytes 37511232 | solution.py:75
  341.5 9.6 %conditional.2 = (f32[512,1,5]{0,2,1:T(8,128)S(1)}, f32[512,1,5]{0,2,1:T(8,128)S(1)}, f32[512,1,5,128]{0,3,2,1:T(8,128)S(1)}) conditional(s32[]{:T(128)} %bitcast.94, (s32[512]{0:T(512)S(1)}, s32[1024]{0:T(1024)S(1)}, s32[1024]{0:T(1024)S(1)}, s32[512]{0:T(512)S(1)}, s32[]{:T(128)}, /*index=5*/bf16[16384,1,128]{2,0,1:T(8,128)(2,1)}, ...), branch_computations={%region_5.6_spmd, %region_8.7_spmd} | conditional | flops 1373249024 | bytes 37511232 | solution.py:75
  356.0 9.6 %conditional.2 = (f32[512,1,5]{0,2,1:T(8,128)S(1)}, f32[512,1,5]{0,2,1:T(8,128)S(1)}, f32[512,1,5,128]{0,3,2,1:T(8,128)S(1)}) conditional(s32[]{:T(128)} %bitcast.94, (s32[512]{0:T(512)S(1)}, s32[1024]{0:T(1024)S(1)}, s32[1024]{0:T(1024)S(1)}, s32[512]{0:T(512)S(1)}, s32[]{:T(128)}, /*index=5*/bf16[16384,1,128]{2,0,1:T(8,128)(2,1)}, ...), branch_computations={%region_5.6_spmd, %region_8.7_spmd} | conditional | flops 1373249024 | bytes 37511232 | solution.py:75
  370.5 9.6 %conditional.2 = (f32[512,1,5]{0,2,1:T(8,128)S(1)}, f32[512,1,5]{0,2,1:T(8,128)S(1)}, f32[512,1,5,128]{0,3,2,1:T(8,128)S(1)}) conditional(s32[]{:T(128)} %bitcast.94, (s32[512]{0:T(512)S(1)}, s32[1024]{0:T(1024)S(1)}, s32[1024]{0:T(1024)S(1)}, s32[512]{0:T(512)S(1)}, s32[]{:T(128)}, /*index=5*/bf16[16384,1,128]{2,0,1:T(8,128)(2,1)}, ...), branch_computations={%region_5.6_spmd, %region_8.7_spmd} | conditional | flops 1373249024 | bytes 37511232 | solution.py:75
  385.0 9.6 %conditional.2 = (f32[512,1,5]{0,2,1:T(8,128)S(1)}, f32[512,1,5]{0,2,1:T(8,128)S(1)}, f32[512,1,5,128]{0,3,2,1:T(8,128)S(1)}) conditional(s32[]{:T(128)} %bitcast.94, (s32[512]{0:T(512)S(1)}, s32[1024]{0:T(1024)S(1)}, s32[1024]{0:T(1024)S(1)}, s32[512]{0:T(512)S(1)}, s32[]{:T(128)}, /*index=5*/bf16[16384,1,128]{2,0,1:T(8,128)(2,1)}, ...), branch_computations={%region_5.6_spmd, %region_8.7_spmd} | conditional | flops 1373249024 | bytes 37511232 | solution.py:75
  399.6 9.6 %conditional.2 = (f32[512,1,5]{0,2,1:T(8,128)S(1)}, f32[512,1,5]{0,2,1:T(8,128)S(1)}, f32[512,1,5,128]{0,3,2,1:T(8,128)S(1)}) conditional(s32[]{:T(128)} %bitcast.94, (s32[512]{0:T(512)S(1)}, s32[1024]{0:T(1024)S(1)}, s32[1024]{0:T(1024)S(1)}, s32[512]{0:T(512)S(1)}, s32[]{:T(128)}, /*index=5*/bf16[16384,1,128]{2,0,1:T(8,128)(2,1)}, ...), branch_computations={%region_5.6_spmd, %region_8.7_spmd} | conditional | flops 1373249024 | bytes 37511232 | solution.py:75
  414.1 9.6 %conditional.2 = (f32[512,1,5]{0,2,1:T(8,128)S(1)}, f32[512,1,5]{0,2,1:T(8,128)S(1)}, f32[512,1,5,128]{0,3,2,1:T(8,128)S(1)}) conditional(s32[]{:T(128)} %bitcast.94, (s32[512]{0:T(512)S(1)}, s32[1024]{0:T(1024)S(1)}, s32[1024]{0:T(1024)S(1)}, s32[512]{0:T(512)S(1)}, s32[]{:T(128)}, /*index=5*/bf16[16384,1,128]{2,0,1:T(8,128)(2,1)}, ...), branch_computations={%region_5.6_spmd, %region_8.7_spmd} | conditional | flops 1373249024 | bytes 37511232 | solution.py:75
  428.6 9.6 %conditional.2 = (f32[512,1,5]{0,2,1:T(8,128)S(1)}, f32[512,1,5]{0,2,1:T(8,128)S(1)}, f32[512,1,5,128]{0,3,2,1:T(8,128)S(1)}) conditional(s32[]{:T(128)} %bitcast.94, (s32[512]{0:T(512)S(1)}, s32[1024]{0:T(1024)S(1)}, s32[1024]{0:T(1024)S(1)}, s32[512]{0:T(512)S(1)}, s32[]{:T(128)}, /*index=5*/bf16[16384,1,128]{2,0,1:T(8,128)(2,1)}, ...), branch_computations={%region_5.6_spmd, %region_8.7_spmd} | conditional | flops 1373249024 | bytes 37511232 | solution.py:75
  443.3 16.0 %all_to_all.44 = bf16[8,128,640]{2,1,0:T(8,128)(2,1)S(1)} all-to-all(bf16[8,128,640]{2,1,0:T(8,128)(2,1)S(1)} %copy.42), channel_id=1, replica_groups=mesh['ctx'=16,'head'=8,'dp'=2] {'head'}, dimensions={0} | all-to-all | bytes 2621440 | tf_op jit(solution)/shard_map/all_to_all | solution.py:119
  (410 shorter events, 311.0 us)
Async XLA Ops:
  6.5 82.1 %all-gather.2.cloned.1.call-start = ((), (), s32[]{:S(2)}) async-start(), calls=%async_computation.3 | async-start | bytes 8912896 | tf_op jit(solution)/shard_map/all_gather | solution.py:110
  57.7 8.6 %copy-start.1 = (s32[8]{0:T(128)S(1)}, s32[8]{0:T(128)}, u32[]{:S(2)}) copy-start(s32[8]{0:T(128)} %param.14) | copy-start | bytes 100
  61.8 20.7 %all-to-all-start = ((bf16[8,2,40960]{2,1,0:T(2,128)(2,1)}), bf16[8,2,40960]{2,1,0:T(2,128)(2,1)}, u32[]{:S(2)}, u32[]{:S(2)}) async-start(bf16[8,2,40960]{2,1,0:T(2,128)(2,1)} %reshape.141), calls=%async_computation | async-start | bytes 2621440 | tf_op jit(solution)/shard_map/all_to_all | solution.py:95
  443.3 16.8 %copy-start = (f32[5120]{0:T(1024)S(1)}, f32[5120]{0:T(1024)}, u32[]{:S(2)}) copy-start(f32[5120]{0:T(1024)} %param.15) | copy-start | bytes 61444
Sparse Core Ops, SparseCore 0:
  23.7 53.6 all-gather.1
where the time goes:
time: 474 us; the launch traced here: 471 us
  matrix products  117 us (25%)
  local copies, waits for them, and re-layouts  116 us (24%)
  other arithmetic  92.2 us (19%)
  loops' own time  81.2 us (17%)
  blocking collectives  30.1 us (6%)
  waiting for transfers between devices  16.1 us (3%)
  between operations  13.5 us (3%)
    another operation x2, loops' own time, query_step(): lax.fori_loop(0, panel_rows // k_block, key_step, partial_value)  79.4 us
    dot_general x18, matrix products, update(): jnp.einsum('qhgk,khd->qhgd', weights.astype(jnp.bfloat16), value_tile, pr...  66 us
    dot_general x18, matrix products, update(): jnp.einsum('qhgd,khd->qhgk', query_tile, key_tile, preferred_element_type...  51 us
    reduce_sum x18, other arithmetic, update(): new_sum = blk_sum * factor + jnp.sum(weights, axis=3)  39.3 us
    unnamed x1, other arithmetic  28.8 us
    slice x32, local copies, waits for them, and re-layouts, key_step(): q_positions[-1]  20.6 us
    slice x32, local copies, waits for them, and re-layouts, key_step(): k_docs[-1] < q_docs[0]  20.6 us
    slice x32, local copies, waits for them, and re-layouts, key_step(): k_positions[0] > q_positions[-1]  16.9 us
  transfers between devices with their start and end apart: 2, of which 1 were waited for; matrix products, arithmetic and copies ran while one was open for 9% of the time, Pallas kernels for 0%

commit v1 on v0

v1 whole, which is shorter than its diff:
```python
import functools
import math

import jax
import jax.numpy as jnp
from jax import lax
from jax.experimental import pallas as pl
from jax.experimental.pallas import tpu as pltpu
from jax.sharding import Mesh
from jax.sharding import PartitionSpec as P

QH = 40
KVH = 8
HD = 128
GROUPS = QH // KVH
NEG = -1e30
LOG2E = 1.4426950408889634
LAYERS = 8
PLANE = 8
SEG = 128
RUN = PLANE * SEG
KEY_TILE = 512


def attend_kernel(place, lengths, q_ref, kv_hbm, steer_ref, o_ref, kv, acc, top, sems):
    ndoc = lengths.shape[0]
    core = place[0]
    slot = place[1]
    tiles_per_run = RUN // KEY_TILE
    scale = HD ** (-0.5) * LOG2E

    def run_copy(run):
        layer, half = run // 2, run % 2
        return pltpu.make_async_copy(
            kv_hbm.at[pl.ds(half * PLANE, PLANE), layer], kv.at[run], sems.at[run]
        )

    for run in range(2 * LAYERS):
        run_copy(run).start()

    ones = jnp.ones((KEY_TILE, HD), jnp.bfloat16)

    def segment(j, _):
        base = (j * 2 + core) * RUN + slot * SEG
        run_copy(2 * j).wait()
        run_copy(2 * j + 1).wait()

        rows = base + lax.broadcasted_iota(jnp.int32, (SEG, 1), 0)
        first_doc = jnp.int32(0)
        last_doc = jnp.int32(0)
        row_doc = jnp.zeros((SEG, 1), jnp.int32)
        bound = jnp.int32(0)
        for d in range(ndoc):
            bound = bound + lengths[d]
            first_doc = jnp.where(bound <= base, bound, first_doc)
            last_doc = jnp.where(bound <= base + SEG - 1, bound, last_doc)
            row_doc = jnp.where(bound <= rows, bound, row_doc)

        acc[...] = jnp.zeros_like(acc)
        top[...] = jnp.full_like(top, NEG)

        def tile(t, masked):
            run = t // tiles_per_run
            part = t % tiles_per_run
            per = KEY_TILE // SEG
            block = kv[run, pl.ds(part * per, per)].reshape(KEY_TILE, 2 * HD)
            keys = block[:, :HD]
            values = jnp.concatenate([block[:, HD:], ones], axis=1)
            if masked:
                cols = t * KEY_TILE + lax.broadcasted_iota(jnp.int32, (1, KEY_TILE), 1)
                visible = (cols <= rows) & (cols >= row_doc)
            for h in range(GROUPS):
                query = q_ref[j, :, h * HD : (h + 1) * HD]
                scores = lax.dot_general(
                    query, keys, (((1,), (1,)), ((), ())), preferred_element_type=jnp.float32
                )
                if masked:
                    scores = jnp.where(visible, scores, NEG)
                old = top[h]
                new = jnp.maximum(old, jnp.max(scores, axis=1, keepdims=True) * scale)
                probs = jnp.exp2(scores * scale - new[:, :1]).astype(jnp.bfloat16)
                factor = jnp.exp2(old - new)
                product = jnp.dot(probs, values, preferred_element_type=jnp.float32)
                acc[h] = acc[h] * jnp.concatenate([factor, factor], axis=1) + product
                top[h] = new

        lo = first_doc // KEY_TILE
        diag = base // KEY_TILE
        full = jnp.minimum((last_doc + KEY_TILE - 1) // KEY_TILE, diag)

        def masked_tile(t, c):
            tile(t, True)
            return c

        def plain_tile(t, c):
            tile(t, False)
            return c

        lax.fori_loop(lo, full, masked_tile, 0)
        lax.fori_loop(full, diag, plain_tile, 0)
        tile(diag, True)

        for h in range(GROUPS):
            both = acc[h]
            attended = (both[:, :HD] / both[:, HD:]).astype(jnp.bfloat16)
            steer = steer_ref[:, h * HD : (h + 1) * HD]
            o_ref[j, :, h * HD : (h + 1) * HD] = (
                attended.astype(jnp.float32) + steer
            ).astype(jnp.bfloat16)
        return 0

    lax.fori_loop(0, LAYERS, segment, 0)


def attend(place, lengths, queries, gathered, steer):
    width = GROUPS * HD
    return pl.pallas_call(
        attend_kernel,
        out_shape=jax.ShapeDtypeStruct((LAYERS, SEG, width), jnp.bfloat16),
        in_specs=[
            pl.BlockSpec(memory_space=pltpu.SMEM),
            pl.BlockSpec(memory_space=pltpu.SMEM),
            pl.BlockSpec(memory_space=pltpu.VMEM),
            pl.BlockSpec(memory_space=pl.ANY),
            pl.BlockSpec(memory_space=pltpu.VMEM),
        ],
        out_specs=pl.BlockSpec(memory_space=pltpu.VMEM),
        scratch_shapes=[
            pltpu.VMEM((2 * LAYERS, PLANE, SEG, 2 * HD), jnp.bfloat16),
            pltpu.VMEM((GROUPS, SEG, 2 * HD), jnp.float32),
            pltpu.VMEM((GROUPS, SEG, HD), jnp.float32),
            pltpu.SemaphoreType.DMA((2 * LAYERS,)),
        ],
        compiler_params=pltpu.CompilerParams(vmem_limit_bytes=48 << 20),
        name="attend",
    )(place, lengths, queries, gathered, steer)


def body(queries, keys, values, doc_lengths, steering):
    tok = queries.shape[0]
    width = GROUPS * HD
    paired = jnp.concatenate(
        (keys.reshape(tok, KVH, HD), values.reshape(tok, KVH, HD)), axis=2
    ).transpose(1, 0, 2)
    kv_local = lax.all_to_all(paired, "z", 0, 0, tiled=True)
    gathered = lax.all_gather(kv_local, ("core", "y", "x"), axis=0, tiled=False)
    wide = queries.reshape(tok, KVH, width).transpose(1, 0, 2)
    wide, kv_local = lax.optimization_barrier((wide, kv_local))
    q_local = lax.all_to_all(wide, "z", 0, 0, tiled=True)
    place = jnp.stack(
        (lax.axis_index("core"), lax.axis_index("y") * 2 + lax.axis_index("x"))
    ).astype(jnp.int32)
    steer = lax.dynamic_slice_in_dim(steering, lax.axis_index("z") * width, width, 0)
    attended = attend(place, doc_lengths, q_local, gathered, steer[None, :])
    back = lax.all_to_all(attended, "z", 0, 0, tiled=True)
    return back.transpose(1, 0, 2).reshape(tok, KVH * width)


def solution(mesh):
    cells = Mesh(
        mesh.devices.reshape(LAYERS, 2, 4, 2, 2), ("z", "core", "y", "x", "dp")
    )
    tokens = P(("dp", "z", "core", "y", "x"), None)
    return jax.shard_map(
        body,
        mesh=cells,
        in_specs=(tokens, tokens, tokens, P("dp"), P()),
        out_specs=tokens,
        check_vma=False,
    )
```

time: 474 us -> 213 us (0.45)
  the two profiles are of different devices: /device:TPU:225 before, /device:TPU:21 now
where the time goes in v1:
time: 213 us; the launch traced here: 212 us
  Pallas kernels  84.1 us (39%)
  blocking collectives  56 us (26%)
  waiting for transfers between devices  46 us (22%)
  between operations  13.5 us (6%)
  local copies, waits for them, and re-layouts  8.55 us (4%)
  starting transfers between devices  3.7 us (2%)
    pallas_call x1, Pallas kernels, attend(): pl.pallas_call(attend_kernel, out_shape=jax.ShapeDtypeStruct((LAYERS, SEG...  84.1 us
    all_to_all x1, waiting for transfers between devices, body(): q_local = lax.all_to_all(wide, 'z', 0, 0, tiled=True)  33.9 us
    all_to_all x1, blocking collectives, body(): back = lax.all_to_all(attended, 'z', 0, 0, tiled=True)  31.9 us
    all_to_all x1, blocking collectives, body(): kv_local = lax.all_to_all(paired, 'z', 0, 0, tiled=True)  24.1 us
    all_gather x1, waiting for transfers between devices, body(): gathered = lax.all_gather(kv_local, ('core', 'y', 'x'), axis=0, tiled=False)  12.2 us
  transfers between devices with their start and end apart: 2, of which 2 were waited for; matrix products, arithmetic and copies ran while one was open for 1% of the time, Pallas kernels for 0%

profile of v1, /device:TPU:21, one launch (start us, length us, event | category | flops | bytes accessed | tf_op | source)
XLA Modules:
  0.0 212.0 jit_solution(3063636181914254221)
XLA Ops:
  6.5 0.0 all-gather.3.cloned.1.call-start
  6.5 1.1 copy.20
  7.7 1.1 copy.21
  8.8 0.0 copy-start.1
  8.8 24.1 %all_to_all.15 = bf16[8,128,256]{1,2,0:T(8,128)(2,1)S(1)} all-to-all(bf16[8,128,256]{1,2,0:T(8,128)(2,1)S(1)} %maximum_bitcast_fusion), channel_id=1, replica_groups=mesh['z'=8,'core'=2,'y'=4,'x'=2,'dp'=2] {'z'}, dimensions={0} | all-to-all | bytes 1048576 | tf_op jit(solution)/shard_map/all_to_all | solution.py:145
  33.0 1.0 copy.22
  34.0 0.0 all-gather.3.cloned.1.call-update
  34.0 0.0 copy-done.1
  34.0 0.8 copy.18
  34.8 1.4 copy.19
  36.3 0.0 copy-start
  36.3 3.7 %all-to-all-start.1 = ((bf16[8,128,640]{2,1,0:T(8,128)(2,1)}), bf16[8,128,640]{2,1,0:T(8,128)(2,1)S(1)}, u32[]{:S(2)}, u32[]{:S(2)}) async-start(bf16[8,128,640]{2,1,0:T(8,128)(2,1)} %bitcast.3), calls=%async_computation.1 | async-start | bytes 2621440 | tf_op jit(solution)/shard_map/all_to_all | solution.py:149
  40.0 0.8 dynamic_slice.3
  40.8 0.1 pad_add_fusion.place
  40.8 33.9 %all-to-all-done.1.q_ref = bf16[8,128,640]{2,1,0:T(8,128)(2,1)S(1)} async-done(((bf16[8,128,640]{2,1,0:T(8,128)(2,1)}), bf16[8,128,640]{2,1,0:T(8,128)(2,1)S(1)}, u32[]{:S(2)}, u32[]{:S(2)}) %all-to-all-start.1) | async-done | bytes 1310752 | tf_op jit(solution)/shard_map/all_to_all | solution.py:149
  74.7 12.2 %all-gather.3.cloned.1.call-done = bf16[128,128,256]{2,1,0:T(8,128)(2,1)} async-done(((bf16[8,128,256]{2,1,0:T(8,128)(2,1)}), bf16[128,128,256]{2,1,0:T(8,128)(2,1)}) %all-gather.3.cloned.1.call-update) | async-done | bytes 8388624 | tf_op jit(solution)/shard_map/all_gather | solution.py:146
  86.9 0.0 copy-done
  86.9 84.1 %attend.1 = bf16[8,128,640]{2,1,0:T(8,128)(2,1)S(1)} custom-call(s32[2]{0:T(128)S(1)} %pad_add_fusion.place, s32[8]{0:T(128)S(1)} %copy-done, bf16[8,128,640]{2,1,0:T(8,128)(2,1)S(1)} %all-to-all-done.1.q_ref, bf16[16,8,128,256]{3,2,1,0:T(8,128)(2,1)} %bitcast.11, f32[1,640]{1,0:T(1,128)S(1)} %broadcast_in_dim.3.steer_ref), custom_call_target="tpu_custom_call" | custom-call | tf_op jit(solution)/shard_map/attend/pallas_call | solution.py:117
  171.0 31.9 %all_to_all.16 = bf16[8,128,640]{2,1,0:T(8,128)(2,1)S(1)} all-to-all(bf16[8,128,640]{2,1,0:T(8,128)(2,1)S(1)} %attend.1), channel_id=1, replica_groups=mesh['z'=8,'core'=2,'y'=4,'x'=2,'dp'=2] {'z'}, dimensions={0} | all-to-all | bytes 2621440 | tf_op jit(solution)/shard_map/all_to_all | solution.py:155
  202.9 0.8 copy.23
  203.7 1.4 copy.24
  (2 shorter events, 0.0 us)
Async XLA Ops:
  6.5 80.3 %all-gather.3.cloned.1.call-start = ((), (), s32[]{:S(2)}) async-start(), calls=%async_computation.3 | async-start | bytes 8912896 | tf_op jit(solution)/shard_map/all_gather | solution.py:146
  8.8 25.2 %copy-start.1 = (bf16[128,5120]{1,0:T(8,128)(2,1)S(1)}, bf16[128,5120]{1,0:T(8,128)(2,1)}, u32[]{:S(2)}) copy-start(bf16[128,5120]{1,0:T(8,128)(2,1)} %param.5) | copy-start | bytes 3932164
  36.3 50.6 %copy-start = (s32[8]{0:T(128)S(1)}, s32[8]{0:T(128)}, u32[]{:S(2)}) copy-start(s32[8]{0:T(128)} %lengths.1) | copy-start | bytes 100
  36.3 38.4 %all-to-all-start.1 = ((bf16[8,128,640]{2,1,0:T(8,128)(2,1)}), bf16[8,128,640]{2,1,0:T(8,128)(2,1)S(1)}, u32[]{:S(2)}, u32[]{:S(2)}) async-start(bf16[8,128,640]{2,1,0:T(8,128)(2,1)} %bitcast.3), calls=%async_computation.1 | async-start | bytes 2621440 | tf_op jit(solution)/shard_map/all_to_all | solution.py:149
Sparse Core Ops, SparseCore 0:
  34.1 52.6 all-gather.2

commit v2 on v1

v2 whole, which is shorter than its diff:
```python
import jax
import jax.numpy as jnp
from jax import lax
from jax.experimental import pallas as pl
from jax.experimental.pallas import tpu as pltpu
from jax.sharding import Mesh
from jax.sharding import PartitionSpec as P

QH = 40
KVH = 8
HD = 128
GROUPS = QH // KVH
WIDTH = GROUPS * HD
NEG = -1e30
LOG2E = 1.4426950408889634
LAYERS = 8
PLANE = 8
SEG = 128
RUN = PLANE * SEG
BLOCKS = 2 * LAYERS * PLANE
ROWS = GROUPS * SEG
PER_TILE = 4
TILE = PER_TILE * SEG
UNROLL = 2
LIMIT = 100.0
PLACES = ((0, 0), (0, 1), (-1, 0), (1, 0), (-1, 1), (1, 1), (2, 0), (2, 1))


EVEN = (4, 2, 6, 0)
ODD = (3, 5, 1, 7)
TURNS = 4


def attend_kernel(place, turns, lengths, q_ref, *refs):
    pieces = refs[:16]
    steer_ref = refs[16]
    number = TURNS
    outs = refs[17 : 17 + number]
    kv, acc, top, qs, high, result, sems = refs[17 + number :]
    ndoc = lengths.shape[0]
    core, row, column, parity = place[0], place[1], place[2], place[3]
    slot = row * 2 + column
    scale = HD ** (-0.5) * LOG2E

    def copies(turn):
        out = []
        for side in range(2):
            for k, (dy, dx) in enumerate(PLACES):
                at_core = (core + side) % 2
                at_slot = ((row + dy + 4) % 4) * 2 + (column + dx) % 2
                n = side * 8 + k
                out.append(
                    pltpu.make_async_copy(
                        pieces[n].at[pl.ds(turn * 2, 2)],
                        kv.at[pl.ds(turn * 2, 2), at_core * PLANE + at_slot],
                        sems.at[turn, n],
                    )
                )
        return out

    for copy in copies(0):
        copy.start()
    ones = jnp.ones((TILE, HD), jnp.bfloat16)

    def wide(x, n):
        return jnp.concatenate([x] * (n // HD), axis=1)

    def segment(turn, _):
        @pl.when(turn + 1 < TURNS)
        def _():
            for copy in copies(turn + 1):
                copy.start()

        j = turn * 2 + parity
        base = (j * 2 + core) * RUN + slot * SEG
        rows = base + lax.broadcasted_iota(jnp.int32, (SEG, 1), 0)
        first = jnp.int32(0)
        row_doc = jnp.zeros((SEG, 1), jnp.int32)
        bound = jnp.int32(0)
        for d in range(ndoc):
            bound = bound + lengths[d]
            first = jnp.where(bound <= base, bound, first)
            row_doc = jnp.where(bound <= rows, bound, row_doc)
        low = first // SEG
        diag = base // SEG
        count = (diag + 1 - low + PER_TILE - 1) // PER_TILE

        for h in range(GROUPS):
            exact = q_ref[j, :, h * HD : (h + 1) * HD].astype(jnp.float32) * scale
            upper = exact.astype(jnp.bfloat16)
            qs[h * SEG : (h + 1) * SEG, :HD] = upper
            qs[h * SEG : (h + 1) * SEG, HD:] = (exact - upper.astype(jnp.float32)).astype(
                jnp.bfloat16
            )

        for copy in copies(turn):
            copy.wait()

        def scores(b, n):
            keys = jnp.concatenate(
                [kv[(b + u) // 16, (b + u) % 16, :HD, :] for u in range(n)], axis=1
            )
            return jnp.dot(
                qs[...],
                jnp.concatenate([keys, keys], axis=0),
                preferred_element_type=jnp.float32,
            )

        def hide(s, b, n, to_key):
            cols = b * SEG + lax.broadcasted_iota(jnp.int32, (1, n * SEG), 1)
            visible = (cols <= jnp.minimum(rows, to_key - 1)) & (cols >= row_doc)
            return jnp.where(
                visible[None], s.reshape(GROUPS, SEG, n * SEG), NEG
            ).reshape(ROWS, n * SEG)

        def tile_at(i):
            end = diag + 1 - i * PER_TILE
            b = jnp.maximum(end - PER_TILE, 0)
            rows_of = jnp.concatenate(
                [kv[(b + u) // 16, (b + u) % 16, HD:, :] for u in range(PER_TILE)], axis=0
            )
            return end * SEG, b, jnp.concatenate([rows_of, ones], axis=1)

        seed = jnp.maximum(diag - 1, 0)
        near = hide(scores(seed, 2), seed, 2, BLOCKS * SEG)
        top[...] = jnp.broadcast_to(jnp.max(near, axis=1, keepdims=True), (ROWS, HD))
        acc[...] = jnp.zeros_like(acc)
        high[...] = jnp.full_like(high, NEG)

        def tile(i):
            to_key, b, values = tile_at(i)
            x = hide(scores(b, PER_TILE) - wide(top[...], TILE), b, PER_TILE, to_key)
            peak = x[:, :HD]
            for u in range(1, PER_TILE):
                peak = jnp.maximum(peak, x[:, u * HD : (u + 1) * HD])
            high[...] = jnp.maximum(
                high[...], jnp.max(peak.reshape(ROWS // 8, 8, HD), axis=0)
            )
            probs = jnp.exp2(x).astype(jnp.bfloat16)
            acc[...] += jnp.dot(probs, values, preferred_element_type=jnp.float32)

        def group(g, c):
            for u in range(UNROLL):
                tile(g * UNROLL + u)
            return c

        def single(i, c):
            tile(i)
            return c

        lax.fori_loop(0, count // UNROLL, group, 0)
        lax.fori_loop((count // UNROLL) * UNROLL, count, single, 0)

        @pl.when(jnp.max(high[...]) > LIMIT)
        def _():
            acc[...] = jnp.zeros_like(acc)

            def again(i, c):
                to_key, b, values = tile_at(i)
                s = hide(scores(b, PER_TILE), b, PER_TILE, to_key)
                old = top[...]
                new = jnp.maximum(old, jnp.max(s, axis=1, keepdims=True))
                factor = jnp.exp2(old - new)
                probs = jnp.exp2(s - wide(new, TILE)).astype(jnp.bfloat16)
                acc[...] = acc[...] * wide(factor, 2 * HD) + jnp.dot(
                    probs, values, preferred_element_type=jnp.float32
                )
                top[...] = new
                return c

            lax.fori_loop(0, count, again, 0)

        for h in range(GROUPS):
            both = acc[h * SEG : (h + 1) * SEG]
            attended = (both[:, :HD] / both[:, HD:]).astype(jnp.bfloat16)
            steer = steer_ref[:, h * HD : (h + 1) * HD]
            result[turn, :, h * HD : (h + 1) * HD] = (
                attended.astype(jnp.float32) + steer
            ).astype(jnp.bfloat16)
        return 0

    lax.fori_loop(0, TURNS, segment, 0)
    for n in range(number):
        outs[n][...] = result[turns[n]]


def attend(place, turns, lengths, queries, pieces, steer):
    smem = pl.BlockSpec(memory_space=pltpu.SMEM)
    vmem = pl.BlockSpec(memory_space=pltpu.VMEM)
    hbm = pl.BlockSpec(memory_space=pltpu.HBM)
    f32, bf16 = jnp.float32, jnp.bfloat16
    number = TURNS
    return pl.pallas_call(
        attend_kernel,
        out_shape=[jax.ShapeDtypeStruct((SEG, WIDTH), bf16)] * number,
        in_specs=[smem, smem, smem, vmem] + [hbm] * 16 + [vmem],
        out_specs=[vmem] * number,
        scratch_shapes=[
            pltpu.VMEM((LAYERS, 2 * PLANE, 2 * HD, SEG), bf16),
            pltpu.VMEM((ROWS, 2 * HD), f32),
            pltpu.VMEM((ROWS, HD), f32),
            pltpu.VMEM((ROWS, 2 * HD), bf16),
            pltpu.VMEM((8, HD), f32),
            pltpu.VMEM((number, SEG, WIDTH), bf16),
            pltpu.SemaphoreType.DMA((TURNS, 16)),
        ],
        compiler_params=pltpu.CompilerParams(vmem_limit_bytes=20 << 20),
        cost_estimate=pl.CostEstimate(
            flops=number * ROWS * 3072 * 8 * HD,
            transcendentals=number * ROWS * 3072,
            bytes_accessed=BLOCKS * 4 * HD * SEG,
        ),
        name="attend",
    )(place, turns, lengths, queries, *pieces, steer)


def assemble_kernel(columns, *refs):
    parts, out = refs[:LAYERS], refs[LAYERS]
    for n in range(LAYERS):
        out[:, pl.ds(pl.multiple_of(columns[n] * WIDTH, HD), WIDTH)] = parts[n][...]


def assemble(columns, parts):
    smem = pl.BlockSpec(memory_space=pltpu.SMEM)
    vmem = pl.BlockSpec(memory_space=pltpu.VMEM)
    return pl.pallas_call(
        assemble_kernel,
        out_shape=jax.ShapeDtypeStruct((SEG, LAYERS * WIDTH), jnp.bfloat16),
        in_specs=[smem] + [vmem] * LAYERS,
        out_specs=vmem,
        name="assemble",
    )(columns, *parts)


def ring(own):
    flip = [(0, 1), (1, 0)]
    up = [(i, (i + 1) % 4) for i in range(4)]
    down = [(i, (i - 1) % 4) for i in range(4)]
    beside = lax.ppermute(own, "x", flip)
    up0 = lax.ppermute(own, "y", up)
    down0 = lax.ppermute(own, "y", down)
    up1 = lax.ppermute(beside, "y", up)
    down1 = lax.ppermute(beside, "y", down)
    far0 = lax.ppermute(up0, "y", up)
    far1 = lax.ppermute(down1, "y", down)
    mine = [own, beside, up0, down0, up1, down1, far0, far1]
    every = mine + [lax.ppermute(b, "core", flip) for b in mine]
    return [pltpu.with_memory_space_constraint(b, pltpu.HBM) for b in every]


def body(queries, keys, values, doc_lengths, steering):
    tok = queries.shape[0]
    paired = jnp.concatenate(
        (
            keys.reshape(tok, KVH, HD).transpose(1, 2, 0),
            values.reshape(tok, KVH, HD).transpose(1, 0, 2),
        ),
        axis=1,
    )
    kv_local = lax.all_to_all(paired, "z", 0, 0, tiled=True)
    large = queries.reshape(tok, KVH, WIDTH).transpose(1, 0, 2)
    large, kv_local = lax.optimization_barrier((large, kv_local))
    q_local = lax.all_to_all(large, "z", 0, 0, tiled=True)
    pieces = ring(kv_local)
    layer = lax.axis_index("z")

    def place(parity):
        return jnp.stack(
            (lax.axis_index("core"), lax.axis_index("y"), lax.axis_index("x"), parity)
        ).astype(jnp.int32)

    steer = lax.dynamic_slice_in_dim(steering, lax.axis_index("z") * WIDTH, WIDTH, 0)
    def send(part, shift):
        if shift == 0:
            return part
        return lax.ppermute(part, "z", [(i, (i + shift) % LAYERS) for i in range(LAYERS)])

    def run(flip, shifts, q):
        turns = (layer + jnp.array(shifts, jnp.int32)) % LAYERS // 2
        return attend(
            place((layer + flip) % 2), turns, doc_lengths, q, pieces, steer[None, :]
        )

    even = run(0, EVEN, q_local)
    sent = [send(p, s) for p, s in zip(even, EVEN)]
    q_again, _ = lax.optimization_barrier((q_local, tuple(even)))
    odd = run(1, ODD, q_again)
    odd, sent = lax.optimization_barrier((tuple(odd), tuple(sent)))
    sent = list(sent) + [send(p, s) for p, s in zip(odd, ODD)]
    columns = (layer - jnp.array(EVEN + ODD, jnp.int32) + LAYERS) % LAYERS
    return assemble(columns, sent)


def solution(mesh):
    cells = Mesh(
        mesh.devices.reshape(LAYERS, 2, 4, 2, 2), ("z", "core", "y", "x", "dp")
    )
    tokens = P(("dp", "z", "core", "y", "x"), None)
    return jax.shard_map(
        body,
        mesh=cells,
        in_specs=(tokens, tokens, tokens, P("dp"), P()),
        out_specs=tokens,
        check_vma=False,
    )
```

time: 213 us -> 152 us (0.71)
  the two profiles are of different devices: /device:TPU:21 before, /device:TPU:1 now
where the time goes in v2:
time: 152 us
  waiting for transfers between devices  53.5 us (35%)
  starting transfers between devices  48.5 us (32%)
  Pallas kernels  40.7 us (27%)
  local copies, waits for them, and re-layouts  7.06 us (5%)
  other arithmetic  1.61 us (1%)
    pallas_call x2, Pallas kernels, attend(): pl.pallas_call(attend_kernel, out_shape=[jax.ShapeDtypeStruct((SEG, WIDTH...  38.1 us
    ppermute x7, starting transfers between devices, send(): lax.ppermute(part, 'z', [(i, (i + shift) % LAYERS) for i in range(LAYERS)])  16.1 us
    all_to_all x1, waiting for transfers between devices, body(): kv_local = lax.all_to_all(paired, 'z', 0, 0, tiled=True)  15.7 us
    ppermute x7, waiting for transfers between devices, send(): lax.ppermute(part, 'z', [(i, (i + shift) % LAYERS) for i in range(LAYERS)])  10.2 us
    ppermute x1, waiting for transfers between devices, ring(): up1 = lax.ppermute(beside, 'y', up)  10 us
    ppermute x8, starting transfers between devices, ring(): every = mine + [lax.ppermute(b, 'core', flip) for b in mine]  9.34 us
    all_to_all x1, starting transfers between devices, body(): kv_local = lax.all_to_all(paired, 'z', 0, 0, tiled=True)  9.01 us
    ppermute x1, waiting for transfers between devices, ring(): beside = lax.ppermute(own, 'x', flip)  8.1 us
  transfers between devices with their start and end apart: 24, of which 11 were waited for; matrix products, arithmetic and copies ran while one was open for 2% of the time, Pallas kernels for 14%

profile of v2, /device:TPU:1, one launch (start us, length us, event | category | flops | bytes accessed | tf_op | source)
XLA Modules:
  0.0 151.6 jit_solution(17280276111122856170)
XLA Ops:
  3.3 9.0 %all-to-all-start = ((bf16[8,256,128]{2,1,0:T(8,128)(2,1)}), bf16[8,256,128]{2,1,0:T(8,128)(2,1)S(1)}, u32[]{:S(2)}, u32[]{:S(2)}) async-start(bf16[8,256,128]{2,1,0:T(8,128)(2,1)} %pad_maximum_fusion), calls=%async_computation | async-start | bytes 1048576 | tf_op jit(solution)/shard_map/all_to_all | solution.py:260
  13.1 1.4 copy.11
  14.5 15.7 %all-to-all-done.refs_0_ = bf16[8,256,128]{2,1,0:T(8,128)(2,1)S(1)} async-done(((bf16[8,256,128]{2,1,0:T(8,128)(2,1)}), bf16[8,256,128]{2,1,0:T(8,128)(2,1)S(1)}, u32[]{:S(2)}, u32[]{:S(2)}) %all-to-all-start) | async-done | bytes 524320 | tf_op jit(solution)/shard_map/all_to_all | solution.py:260
  30.3 3.7 %all-to-all-start.1 = ((bf16[8,128,640]{2,1,0:T(8,128)(2,1)}), bf16[8,128,640]{2,1,0:T(8,128)(2,1)S(1)}, u32[]{:S(2)}, u32[]{:S(2)}) async-start(bf16[8,128,640]{2,1,0:T(8,128)(2,1)} %bitcast.5), calls=%async_computation.1 | async-start | bytes 2621440 | tf_op jit(solution)/shard_map/all_to_all | solution.py:263
  35.3 2.7 %collective-permute-start.2 = (bf16[8,256,128]{2,1,0:T(8,128)(2,1)S(1)}, bf16[8,256,128]{2,1,0:T(8,128)(2,1)}, u32[]{:S(2)}, u32[]{:S(2)}) collective-permute-start(bf16[8,256,128]{2,1,0:T(8,128)(2,1)S(1)} %all-to-all-done.refs_0_), channel_id=1, source_target_pairs={{0,12},{4,0},{8,4},{12,8},{1,13},{5,1},{9,5},{13,9},{2,14},{6,2},{... | collective-permute-start | bytes 1572872 | tf_op jit(solution)/shard_map/ppermute | solution.py:241
  39.1 8.1 %collective-permute-done.refs_1_ = bf16[8,256,128]{2,1,0:T(8,128)(2,1)S(1)} collective-permute-done((bf16[8,256,128]{2,1,0:T(8,128)(2,1)S(1)}, bf16[8,256,128]{2,1,0:T(8,128)(2,1)S(1)}, u32[]{:S(2)}, u32[]{:S(2)}) %collective-permute-start) | collective-permute-done | bytes 524320 | tf_op jit(solution)/shard_map/ppermute | solution.py:239
  47.2 2.7 %collective-permute-start.4 = (bf16[8,256,128]{2,1,0:T(8,128)(2,1)S(1)}, bf16[8,256,128]{2,1,0:T(8,128)(2,1)}, u32[]{:S(2)}, u32[]{:S(2)}) collective-permute-start(bf16[8,256,128]{2,1,0:T(8,128)(2,1)S(1)} %collective-permute-done.refs_1_), channel_id=1, source_target_pairs={{0,12},{4,0},{8,4},{12,8},{1,13},{5,1},{9,5},{13,9},{2,14},{6,2},{... | collective-permute-start | bytes 1572872 | tf_op jit(solution)/shard_map/ppermute | solution.py:243
  49.9 1.5 collective-permute-start.10
  51.7 2.0 %collective-permute-start.9 = (bf16[8,256,128]{2,1,0:T(8,128)(2,1)}, bf16[8,256,128]{2,1,0:T(8,128)(2,1)}, u32[]{:S(2)}, u32[]{:S(2)}) collective-permute-start(bf16[8,256,128]{2,1,0:T(8,128)(2,1)} %collective-permute-done.1.refs_2_), channel_id=1, source_target_pairs={{0,16},{16,0},{1,17},{17,1},{2,18},{18,2},{3,19},{19,3},{4,20},{20... | collective-permute-start | bytes 1572872 | tf_op jit(solution)/shard_map/ppermute | solution.py:247
  53.8 6.1 %collective-permute-done.4.refs_5_ = bf16[8,256,128]{2,1,0:T(8,128)(2,1)} collective-permute-done((bf16[8,256,128]{2,1,0:T(8,128)(2,1)S(1)}, bf16[8,256,128]{2,1,0:T(8,128)(2,1)}, u32[]{:S(2)}, u32[]{:S(2)}) %collective-permute-start.4) | collective-permute-done | bytes 524320 | tf_op jit(solution)/shard_map/ppermute | solution.py:243
  59.9 3.5 %collective-permute-start.6 = (bf16[8,256,128]{2,1,0:T(8,128)(2,1)}, bf16[8,256,128]{2,1,0:T(8,128)(2,1)S(1)}, u32[]{:S(2)}, u32[]{:S(2)}) collective-permute-start(bf16[8,256,128]{2,1,0:T(8,128)(2,1)} %collective-permute-done.4.refs_5_), channel_id=1, source_target_pairs={{0,12},{4,0},{8,4},{12,8},{1,13},{5,1},{9,5},{13,9},{2,14},{6,2},{... | collective-permute-start | bytes 1572872 | tf_op jit(solution)/shard_map/ppermute | solution.py:245
  64.2 2.5 %collective-permute-start.8 = (bf16[8,256,128]{2,1,0:T(8,128)(2,1)S(1)}, bf16[8,256,128]{2,1,0:T(8,128)(2,1)S(1)}, u32[]{:S(2)}, u32[]{:S(2)}) collective-permute-start(bf16[8,256,128]{2,1,0:T(8,128)(2,1)S(1)} %collective-permute-done.refs_1_), channel_id=1, source_target_pairs={{0,16},{16,0},{1,17},{17,1},{2,18},{18,2},{3,19},{19,3},{4,20},{20... | collective-permute-start | bytes 1572872 | tf_op jit(solution)/shard_map/ppermute | solution.py:247
  66.9 1.9 %collective-permute-done.5.refs_6_ = bf16[8,256,128]{2,1,0:T(8,128)(2,1)} collective-permute-done((bf16[8,256,128]{2,1,0:T(8,128)(2,1)}, bf16[8,256,128]{2,1,0:T(8,128)(2,1)}, u32[]{:S(2)}, u32[]{:S(2)}) %collective-permute-start.5) | collective-permute-done | bytes 524320 | tf_op jit(solution)/shard_map/ppermute | solution.py:244
  69.9 10.0 %collective-permute-done.3.refs_4_ = bf16[8,256,128]{2,1,0:T(8,128)(2,1)S(1)} collective-permute-done((bf16[8,256,128]{2,1,0:T(8,128)(2,1)S(1)}, bf16[8,256,128]{2,1,0:T(8,128)(2,1)S(1)}, u32[]{:S(2)}, u32[]{:S(2)}) %collective-permute-start.3) | collective-permute-done | bytes 524320 | tf_op jit(solution)/shard_map/ppermute | solution.py:242
  83.2 17.1 %attend.2 = (bf16[128,640]{1,0:T(8,128)(2,1)S(1)}, bf16[128,640]{1,0:T(8,128)(2,1)S(1)}, bf16[128,640]{1,0:T(8,128)(2,1)S(1)}, bf16[128,640]{1,0:T(8,128)(2,1)S(1)}) custom-call(s32[4]{0:T(128)S(1)} %get-tuple-element.43.place, s32[4]{0:T(128)S(1)} %and_select_fusion.turns, s32[8]{0:T(128)S(1)} %copy-done.1, bf16[8,128,640]{2,1,0:T(8,128)(2,1)S(1)} %all-to-all-done.1.q_ref, ...), custom_call_target="tpu_custom_call" | custom-call | flops 8053063680 | bytes 8388608 | tf_op jit(solution)/shard_map/attend/pallas_call | solution.py:193
  100.4 5.3 %collective-permute-start.15 = (bf16[128,640]{1,0:T(8,128)(2,1)S(1)}, bf16[128,640]{1,0:T(8,128)(2,1)S(1)}, u32[]{:S(2)}, u32[]{:S(2)}) collective-permute-start(bf16[128,640]{1,0:T(8,128)(2,1)S(1)} %get-tuple-element.26), channel_id=1, source_target_pairs={{0,128},{32,160},{64,192},{96,224},{128,0},{160,32},{192,64},{224,... | collective-permute-start | bytes 491528 | tf_op jit(solution)/shard_map/ppermute | solution.py:276
  105.9 3.3 %collective-permute-start.17 = (bf16[128,640]{1,0:T(8,128)(2,1)S(1)}, bf16[128,640]{1,0:T(8,128)(2,1)S(1)}, u32[]{:S(2)}, u32[]{:S(2)}) collective-permute-start(bf16[128,640]{1,0:T(8,128)(2,1)S(1)} %get-tuple-element.28), channel_id=1, source_target_pairs={{0,192},{32,224},{64,0},{96,32},{128,64},{160,96},{192,128},{224,1... | collective-permute-start | bytes 491528 | tf_op jit(solution)/shard_map/ppermute | solution.py:276
  109.2 21.0 %attend.3 = (bf16[128,640]{1,0:T(8,128)(2,1)S(1)}, bf16[128,640]{1,0:T(8,128)(2,1)S(1)}, bf16[128,640]{1,0:T(8,128)(2,1)S(1)}, bf16[128,640]{1,0:T(8,128)(2,1)S(1)}) custom-call(s32[4]{0:T(128)S(1)} %pad_add_fusion.place, s32[4]{0:T(128)S(1)} %and_select_fusion.2.turns, s32[8]{0:T(128)S(1)} %copy-done.1, bf16[8,128,640]{2,1,0:T(8,128)(2,1)S(1)} %all-to-all-done.1.q_ref, ...), custom_call_target="tpu_custom_call" | custom-call | flops 8053063680 | bytes 8388608 | tf_op jit(solution)/shard_map/attend/pallas_call | solution.py:193
  130.4 4.5 %collective-permute-start.19 = (bf16[128,640]{1,0:T(8,128)(2,1)S(1)}, bf16[128,640]{1,0:T(8,128)(2,1)S(1)}, u32[]{:S(2)}, u32[]{:S(2)}) collective-permute-start(bf16[128,640]{1,0:T(8,128)(2,1)S(1)} %get-tuple-element.40), channel_id=1, source_target_pairs={{0,160},{32,192},{64,224},{96,0},{128,32},{160,64},{192,96},{224,1... | collective-permute-start | bytes 491528 | tf_op jit(solution)/shard_map/ppermute | solution.py:276
  135.1 2.4 %collective-permute-start.21 = (bf16[128,640]{1,0:T(8,128)(2,1)S(1)}, bf16[128,640]{1,0:T(8,128)(2,1)S(1)}, u32[]{:S(2)}, u32[]{:S(2)}) collective-permute-start(bf16[128,640]{1,0:T(8,128)(2,1)S(1)} %get-tuple-element.42), channel_id=1, source_target_pairs={{0,224},{32,0},{64,32},{96,64},{128,96},{160,128},{192,160},{224,1... | collective-permute-start | bytes 491528 | tf_op jit(solution)/shard_map/ppermute | solution.py:276
  138.1 2.8 %collective-permute-done.18.refs_4_ = bf16[128,640]{1,0:T(8,128)(2,1)S(1)} collective-permute-done((bf16[128,640]{1,0:T(8,128)(2,1)S(1)}, bf16[128,640]{1,0:T(8,128)(2,1)S(1)}, u32[]{:S(2)}, u32[]{:S(2)}) %collective-permute-start.18) | collective-permute-done | bytes 163872 | tf_op jit(solution)/shard_map/ppermute | solution.py:276
  140.9 3.9 %collective-permute-done.19.refs_5_ = bf16[128,640]{1,0:T(8,128)(2,1)S(1)} collective-permute-done((bf16[128,640]{1,0:T(8,128)(2,1)S(1)}, bf16[128,640]{1,0:T(8,128)(2,1)S(1)}, u32[]{:S(2)}, u32[]{:S(2)}) %collective-permute-start.19) | collective-permute-done | bytes 163872 | tf_op jit(solution)/shard_map/ppermute | solution.py:276
  145.7 2.7 %collective-permute-done.21.refs_7_ = bf16[128,640]{1,0:T(8,128)(2,1)S(1)} collective-permute-done((bf16[128,640]{1,0:T(8,128)(2,1)S(1)}, bf16[128,640]{1,0:T(8,128)(2,1)S(1)}, u32[]{:S(2)}, u32[]{:S(2)}) %collective-permute-start.21) | collective-permute-done | bytes 163872 | tf_op jit(solution)/shard_map/ppermute | solution.py:276
  149.1 2.6 %assemble.1 = bf16[128,5120]{1,0:T(8,128)(2,1)} custom-call(s32[8]{0:T(128)} %and_select_fusion.4.columns, bf16[128,640]{1,0:T(8,128)(2,1)} %copy-done.4, bf16[128,640]{1,0:T(8,128)(2,1)} %copy-done.5, bf16[128,640]{1,0:T(8,128)(2,1)} %copy-done.6, bf16[128,640]{1,0:T(8,128)(2,1)} %copy-done, bf16[128,640]{1,0:T(8,128)(2,1)} %copy-done.7, ...), custom_call_target="tpu_custom_call" | custom-call | tf_op jit(solution)/shard_map/assemble/pallas_call | solution.py:226
  (84 shorter events, 14.7 us)
Async XLA Ops:
  3.3 27.0 %all-to-all-start = ((bf16[8,256,128]{2,1,0:T(8,128)(2,1)}), bf16[8,256,128]{2,1,0:T(8,128)(2,1)S(1)}, u32[]{:S(2)}, u32[]{:S(2)}) async-start(bf16[8,256,128]{2,1,0:T(8,128)(2,1)} %pad_maximum_fusion), calls=%async_computation | async-start | bytes 1048576 | tf_op jit(solution)/shard_map/all_to_all | solution.py:260
  30.3 52.9 %all-to-all-start.1 = ((bf16[8,128,640]{2,1,0:T(8,128)(2,1)}), bf16[8,128,640]{2,1,0:T(8,128)(2,1)S(1)}, u32[]{:S(2)}, u32[]{:S(2)}) async-start(bf16[8,128,640]{2,1,0:T(8,128)(2,1)} %bitcast.5), calls=%async_computation.1 | async-start | bytes 2621440 | tf_op jit(solution)/shard_map/all_to_all | solution.py:263
  34.0 13.2 %collective-permute-start = (bf16[8,256,128]{2,1,0:T(8,128)(2,1)S(1)}, bf16[8,256,128]{2,1,0:T(8,128)(2,1)S(1)}, u32[]{:S(2)}, u32[]{:S(2)}) collective-permute-start(bf16[8,256,128]{2,1,0:T(8,128)(2,1)S(1)} %all-to-all-done.refs_0_), channel_id=1, source_target_pairs={{0,2},{2,0},{1,3},{3,1},{4,6},{6,4},{5,7},{7,5},{8,10},{10,8},{9,1... | collective-permute-start | bytes 1572872 | tf_op jit(solution)/shard_map/ppermute | solution.py:239
  35.3 14.6 %collective-permute-start.2 = (bf16[8,256,128]{2,1,0:T(8,128)(2,1)S(1)}, bf16[8,256,128]{2,1,0:T(8,128)(2,1)}, u32[]{:S(2)}, u32[]{:S(2)}) collective-permute-start(bf16[8,256,128]{2,1,0:T(8,128)(2,1)S(1)} %all-to-all-done.refs_0_), channel_id=1, source_target_pairs={{0,12},{4,0},{8,4},{12,8},{1,13},{5,1},{9,5},{13,9},{2,14},{6,2},{... | collective-permute-start | bytes 1572872 | tf_op jit(solution)/shard_map/ppermute | solution.py:241
  38.0 13.7 %collective-permute-start.1 = (bf16[8,256,128]{2,1,0:T(8,128)(2,1)S(1)}, bf16[8,256,128]{2,1,0:T(8,128)(2,1)}, u32[]{:S(2)}, u32[]{:S(2)}) collective-permute-start(bf16[8,256,128]{2,1,0:T(8,128)(2,1)S(1)} %all-to-all-done.refs_0_), channel_id=1, source_target_pairs={{0,4},{4,8},{8,12},{12,0},{1,5},{5,9},{9,13},{13,1},{2,6},{6,10},{... | collective-permute-start | bytes 1572872 | tf_op jit(solution)/shard_map/ppermute | solution.py:240
  38.0 15.7 %collective-permute-start.7 = (bf16[8,256,128]{2,1,0:T(8,128)(2,1)S(1)}, bf16[8,256,128]{2,1,0:T(8,128)(2,1)S(1)}, u32[]{:S(2)}, u32[]{:S(2)}) collective-permute-start(bf16[8,256,128]{2,1,0:T(8,128)(2,1)S(1)} %all-to-all-done.refs_0_), channel_id=1, source_target_pairs={{0,16},{16,0},{1,17},{17,1},{2,18},{18,2},{3,19},{19,3},{4,20},{20... | collective-permute-start | bytes 1572872 | tf_op jit(solution)/shard_map/ppermute | solution.py:247
  47.2 12.7 %collective-permute-start.4 = (bf16[8,256,128]{2,1,0:T(8,128)(2,1)S(1)}, bf16[8,256,128]{2,1,0:T(8,128)(2,1)}, u32[]{:S(2)}, u32[]{:S(2)}) collective-permute-start(bf16[8,256,128]{2,1,0:T(8,128)(2,1)S(1)} %collective-permute-done.refs_1_), channel_id=1, source_target_pairs={{0,12},{4,0},{8,4},{12,8},{1,13},{5,1},{9,5},{13,9},{2,14},{6,2},{... | collective-permute-start | bytes 1572872 | tf_op jit(solution)/shard_map/ppermute | solution.py:243
  49.9 14.3 %collective-permute-start.10 = (bf16[8,256,128]{2,1,0:T(8,128)(2,1)}, bf16[8,256,128]{2,1,0:T(8,128)(2,1)}, u32[]{:S(2)}, u32[]{:S(2)}) collective-permute-start(bf16[8,256,128]{2,1,0:T(8,128)(2,1)} %collective-permute-done.2.refs_3_), channel_id=1, source_target_pairs={{0,16},{16,0},{1,17},{17,1},{2,18},{18,2},{3,19},{19,3},{4,20},{20... | collective-permute-start | bytes 1572872 | tf_op jit(solution)/shard_map/ppermute | solution.py:247
  51.7 15.1 %collective-permute-start.9 = (bf16[8,256,128]{2,1,0:T(8,128)(2,1)}, bf16[8,256,128]{2,1,0:T(8,128)(2,1)}, u32[]{:S(2)}, u32[]{:S(2)}) collective-permute-start(bf16[8,256,128]{2,1,0:T(8,128)(2,1)} %collective-permute-done.1.refs_2_), channel_id=1, source_target_pairs={{0,16},{16,0},{1,17},{17,1},{2,18},{18,2},{3,19},{19,3},{4,20},{20... | collective-permute-start | bytes 1572872 | tf_op jit(solution)/shard_map/ppermute | solution.py:247
  53.7 15.1 %collective-permute-start.5 = (bf16[8,256,128]{2,1,0:T(8,128)(2,1)}, bf16[8,256,128]{2,1,0:T(8,128)(2,1)}, u32[]{:S(2)}, u32[]{:S(2)}) collective-permute-start(bf16[8,256,128]{2,1,0:T(8,128)(2,1)} %collective-permute-done.1.refs_2_), channel_id=1, source_target_pairs={{0,4},{4,8},{8,12},{12,0},{1,5},{5,9},{9,13},{13,1},{2,6},{6,10},{... | collective-permute-start | bytes 1572872 | tf_op jit(solution)/shard_map/ppermute | solution.py:244
  53.7 26.2 %collective-permute-start.3 = (bf16[8,256,128]{2,1,0:T(8,128)(2,1)S(1)}, bf16[8,256,128]{2,1,0:T(8,128)(2,1)S(1)}, u32[]{:S(2)}, u32[]{:S(2)}) collective-permute-start(bf16[8,256,128]{2,1,0:T(8,128)(2,1)S(1)} %collective-permute-done.refs_1_), channel_id=1, source_target_pairs={{0,4},{4,8},{8,12},{12,0},{1,5},{5,9},{9,13},{13,1},{2,6},{6,10},{... | collective-permute-start | bytes 1572872 | tf_op jit(solution)/shard_map/ppermute | solution.py:242
  59.9 20.8 %collective-permute-start.6 = (bf16[8,256,128]{2,1,0:T(8,128)(2,1)}, bf16[8,256,128]{2,1,0:T(8,128)(2,1)S(1)}, u32[]{:S(2)}, u32[]{:S(2)}) collective-permute-start(bf16[8,256,128]{2,1,0:T(8,128)(2,1)} %collective-permute-done.4.refs_5_), channel_id=1, source_target_pairs={{0,12},{4,0},{8,4},{12,8},{1,13},{5,1},{9,5},{13,9},{2,14},{6,2},{... | collective-permute-start | bytes 1572872 | tf_op jit(solution)/shard_map/ppermute | solution.py:245
  64.2 16.9 %collective-permute-start.8 = (bf16[8,256,128]{2,1,0:T(8,128)(2,1)S(1)}, bf16[8,256,128]{2,1,0:T(8,128)(2,1)S(1)}, u32[]{:S(2)}, u32[]{:S(2)}) collective-permute-start(bf16[8,256,128]{2,1,0:T(8,128)(2,1)S(1)} %collective-permute-done.refs_1_), channel_id=1, source_target_pairs={{0,16},{16,0},{1,17},{17,1},{2,18},{18,2},{3,19},{19,3},{4,20},{20... | collective-permute-start | bytes 1572872 | tf_op jit(solution)/shard_map/ppermute | solution.py:247
  66.8 14.4 %collective-permute-start.12 = (bf16[8,256,128]{2,1,0:T(8,128)(2,1)}, bf16[8,256,128]{2,1,0:T(8,128)(2,1)S(1)}, u32[]{:S(2)}, u32[]{:S(2)}) collective-permute-start(bf16[8,256,128]{2,1,0:T(8,128)(2,1)} %collective-permute-done.4.refs_5_), channel_id=1, source_target_pairs={{0,16},{16,0},{1,17},{17,1},{2,18},{18,2},{3,19},{19,3},{4,20},{20... | collective-permute-start | bytes 1572872 | tf_op jit(solution)/shard_map/ppermute | solution.py:247
  68.8 12.4 %collective-permute-start.13 = (bf16[8,256,128]{2,1,0:T(8,128)(2,1)}, bf16[8,256,128]{2,1,0:T(8,128)(2,1)S(1)}, u32[]{:S(2)}, u32[]{:S(2)}) collective-permute-start(bf16[8,256,128]{2,1,0:T(8,128)(2,1)} %collective-permute-done.5.refs_6_), channel_id=1, source_target_pairs={{0,16},{16,0},{1,17},{17,1},{2,18},{18,2},{3,19},{19,3},{4,20},{20... | collective-permute-start | bytes 1572872 | tf_op jit(solution)/shard_map/ppermute | solution.py:247
  79.9 2.3 %collective-permute-start.11 = (bf16[8,256,128]{2,1,0:T(8,128)(2,1)S(1)}, bf16[8,256,128]{2,1,0:T(8,128)(2,1)S(1)}, u32[]{:S(2)}, u32[]{:S(2)}) collective-permute-start(bf16[8,256,128]{2,1,0:T(8,128)(2,1)S(1)} %collective-permute-done.3.refs_4_), channel_id=1, source_target_pairs={{0,16},{16,0},{1,17},{17,1},{2,18},{18,2},{3,19},{19,3},{4,20},{20... | collective-permute-start | bytes 1572872 | tf_op jit(solution)/shard_map/ppermute | solution.py:247
  80.7 2.5 %collective-permute-start.14 = (bf16[8,256,128]{2,1,0:T(8,128)(2,1)S(1)}, bf16[8,256,128]{2,1,0:T(8,128)(2,1)}, u32[]{:S(2)}, u32[]{:S(2)}) collective-permute-start(bf16[8,256,128]{2,1,0:T(8,128)(2,1)S(1)} %collective-permute-done.6.refs_7_), channel_id=1, source_target_pairs={{0,16},{16,0},{1,17},{17,1},{2,18},{18,2},{3,19},{19,3},{4,20},{20... | collective-permute-start | bytes 1572872 | tf_op jit(solution)/shard_map/ppermute | solution.py:247
  100.4 29.9 %collective-permute-start.15 = (bf16[128,640]{1,0:T(8,128)(2,1)S(1)}, bf16[128,640]{1,0:T(8,128)(2,1)S(1)}, u32[]{:S(2)}, u32[]{:S(2)}) collective-permute-start(bf16[128,640]{1,0:T(8,128)(2,1)S(1)} %get-tuple-element.26), channel_id=1, source_target_pairs={{0,128},{32,160},{64,192},{96,224},{128,0},{160,32},{192,64},{224,... | collective-permute-start | bytes 491528 | tf_op jit(solution)/shard_map/ppermute | solution.py:276
  105.7 24.6 %collective-permute-start.16 = (bf16[128,640]{1,0:T(8,128)(2,1)S(1)}, bf16[128,640]{1,0:T(8,128)(2,1)S(1)}, u32[]{:S(2)}, u32[]{:S(2)}) collective-permute-start(bf16[128,640]{1,0:T(8,128)(2,1)S(1)} %get-tuple-element.27), channel_id=1, source_target_pairs={{0,64},{32,96},{64,128},{96,160},{128,192},{160,224},{192,0},{224,... | collective-permute-start | bytes 491528 | tf_op jit(solution)/shard_map/ppermute | solution.py:276
  105.9 24.4 %collective-permute-start.17 = (bf16[128,640]{1,0:T(8,128)(2,1)S(1)}, bf16[128,640]{1,0:T(8,128)(2,1)S(1)}, u32[]{:S(2)}, u32[]{:S(2)}) collective-permute-start(bf16[128,640]{1,0:T(8,128)(2,1)S(1)} %get-tuple-element.28), channel_id=1, source_target_pairs={{0,192},{32,224},{64,0},{96,32},{128,64},{160,96},{192,128},{224,1... | collective-permute-start | bytes 491528 | tf_op jit(solution)/shard_map/ppermute | solution.py:276
  130.3 10.6 %collective-permute-start.18 = (bf16[128,640]{1,0:T(8,128)(2,1)S(1)}, bf16[128,640]{1,0:T(8,128)(2,1)S(1)}, u32[]{:S(2)}, u32[]{:S(2)}) collective-permute-start(bf16[128,640]{1,0:T(8,128)(2,1)S(1)} %get-tuple-element.39), channel_id=1, source_target_pairs={{0,96},{32,128},{64,160},{96,192},{128,224},{160,0},{192,32},{224,... | collective-permute-start | bytes 491528 | tf_op jit(solution)/shard_map/ppermute | solution.py:276
  130.4 14.4 %collective-permute-start.19 = (bf16[128,640]{1,0:T(8,128)(2,1)S(1)}, bf16[128,640]{1,0:T(8,128)(2,1)S(1)}, u32[]{:S(2)}, u32[]{:S(2)}) collective-permute-start(bf16[128,640]{1,0:T(8,128)(2,1)S(1)} %get-tuple-element.40), channel_id=1, source_target_pairs={{0,160},{32,192},{64,224},{96,0},{128,32},{160,64},{192,96},{224,1... | collective-permute-start | bytes 491528 | tf_op jit(solution)/shard_map/ppermute | solution.py:276
  134.9 10.8 %collective-permute-start.20 = (bf16[128,640]{1,0:T(8,128)(2,1)S(1)}, bf16[128,640]{1,0:T(8,128)(2,1)S(1)}, u32[]{:S(2)}, u32[]{:S(2)}) collective-permute-start(bf16[128,640]{1,0:T(8,128)(2,1)S(1)} %get-tuple-element.41), channel_id=1, source_target_pairs={{0,32},{32,64},{64,96},{96,128},{128,160},{160,192},{192,224},{224... | collective-permute-start | bytes 491528 | tf_op jit(solution)/shard_map/ppermute | solution.py:276
  135.1 13.2 %collective-permute-start.21 = (bf16[128,640]{1,0:T(8,128)(2,1)S(1)}, bf16[128,640]{1,0:T(8,128)(2,1)S(1)}, u32[]{:S(2)}, u32[]{:S(2)}) collective-permute-start(bf16[128,640]{1,0:T(8,128)(2,1)S(1)} %get-tuple-element.42), channel_id=1, source_target_pairs={{0,224},{32,0},{64,32},{96,64},{128,96},{160,128},{192,160},{224,1... | collective-permute-start | bytes 491528 | tf_op jit(solution)/shard_map/ppermute | solution.py:276
  (22 other events, 334.5 us)
